TPU v7x, 32 devices: a whole 2x2x4 slice. The times are simulated.
32 devices in a mesh: lon: 8 (over y, x, core), lat: 4 (over z).
Axes of the slice: x: 2, y: 2, z: 4, core: 2. Of those that a mesh axis runs over, the one named last changes fastest.
Arguments:
- ensemble: float32 [8, 4, 80, 32, 256], P('lon', 'lat'), may hold values from -6 to 6
- obs_block: int32 [3, 128], replicated, may hold values from 0 to 31, as said below
- obs_column: int32 [3, 128], replicated, may hold values from 0 to 255
- obs_value: float32 [3, 128], replicated, may hold values from -8 to 8
- obs_error: float32 [3, 128], replicated, may hold values from 0.5 to 2
- loc_mask: int32 [8, 4, 3, 128, 256], P('lon', 'lat'), may hold values from 0 to 1, as said below
Outputs:
- analysis: float32 [8, 4, 80, 32, 256], P('lon', 'lat')
Inputs may be any that keep to these rules, and one draw needn't show every extreme that they name: `obs_block`: observations fall more often on blocks of low index. `loc_mask`: an observation may update only columns of its own block and of blocks at most two blocks away along longitude (cyclically) and latitude; all other blocks have zeros for it.
All inputs are finite; a program needn't handle non-finite values.
Results may differ from a plain program's by a relative error of at most 0.0001.
Values sent between devices are 32-bit elements; how exact they have to be, the bound alone decides.
No kernel may reach another device: no remote copies, remote signals or barrier semaphores. Data moves between devices by JAX's collectives and lax.ppermute only.
A program may use at most 64 MiB of HBM per device.

v0:
```python
import jax
import jax.numpy as jnp
from jax import lax
from jax.sharding import PartitionSpec as P


def solve_rows(whitened, innov_raw):
    count = whitened.shape[0]
    cmat = jnp.eye(count, dtype=jnp.float32) + jnp.dot(
        whitened, whitened.T, precision=lax.Precision.HIGHEST
    )
    chol = jnp.linalg.cholesky(cmat)
    gain_rows = jax.scipy.linalg.cho_solve((chol, True), whitened)
    innov = jax.scipy.linalg.cho_solve((chol, True), innov_raw)
    return (gain_rows, innov)


def body(ensemble, obs_block, obs_column, obs_value, obs_error, loc_mask):
    members = ensemble.shape[2]
    levels = ensemble.shape[3]
    columns = ensemble.shape[4]
    count = obs_block.shape[1]
    scale = 1.0 / jnp.sqrt(jnp.float32(members - 1))
    n_lat = lax.axis_size("lat")
    lat_here = lax.axis_index("lat")
    state = ensemble.reshape(members, levels * columns)
    col_ids = jnp.arange(columns, dtype=jnp.int32)
    for batch in range(obs_block.shape[0]):
        blocks = obs_block[batch]
        pick = obs_column[batch][:, None] == col_ids[None, :]
        surface = state[:, :columns]
        piece = lax.all_gather(surface[None], "lon", axis=0, tiled=True)
        width = piece.shape[0]
        ids = jnp.arange(width, dtype=jnp.int32) * n_lat + lat_here
        select = ((blocks[:, None] == ids[None, :])[:, :, None] & pick[:, None, :]).astype(
            jnp.float32
        )
        row_part = jnp.zeros((count, members), jnp.float32) + jnp.einsum(
            "pkc,kmc->pm", select, piece, precision=lax.Precision.HIGHEST
        )
        obs_ens = lax.psum(row_part, "lat")
        obs_mean = jnp.mean(obs_ens, axis=1)
        errors = obs_error[batch]
        whitened = (obs_ens - obs_mean[:, None]) * scale / errors[:, None]
        innov_raw = (obs_value[batch] - obs_mean) / errors
        gain_rows, innov = solve_rows(whitened, innov_raw)
        coef = jnp.concatenate([-0.5 * gain_rows.T, (innov * scale)[None, :]], axis=0)
        weights = loc_mask[0, 0, batch].astype(jnp.float32)
        mean = jnp.mean(state, axis=0)
        pert = state - mean[None, :]
        proj = jnp.dot(whitened, pert, precision=lax.Precision.HIGHEST)
        proj = (proj.reshape(count, levels, columns) * weights[:, None, :]).reshape(
            count, levels * columns
        )
        incr = jnp.dot(coef, proj, precision=lax.Precision.HIGHEST)
        state = pert + incr[:members] + (mean + incr[members])[None, :]
    return state.reshape(ensemble.shape)


def solution(mesh):
    placed = (
        P("lon", "lat", None, None, None),
        P(),
        P(),
        P(),
        P(),
        P("lon", "lat", None, None, None),
    )
    return jax.shard_map(
        body,
        mesh=mesh,
        in_specs=placed,
        out_specs=P("lon", "lat", None, None, None),
        check_vma=False,
    )
```

profile of v0, /device:TPU:0, one launch (start us, length us, event | category | flops | bytes accessed | tf_op | source)
XLA Modules:
  0.0 211.4 jit_solution(10639633567476785206)
XLA Ops:
  0.0 0.8 slice_bitcast_fusion.2
  0.9 3.4 %copy.32 = f32[10,8,32,256]{3,1,2,0:T(8,128)S(1)} copy(f32[10,8,32,256]{3,2,1,0:T(8,128)} %bitcast.215) | data formatting | bytes 5242880
  4.3 11.6 %all-gather = f32[640,256]{1,0:T(8,128)S(1)} all-gather(f32[80,256]{1,0:T(8,128)S(1)} %slice.116), channel_id=2, replica_groups=mesh['lon'=8,'lat'=4] {'lon'}, dimensions={0}, use_global_device_ids=true | all-gather | bytes 737280 | tf_op jit(solution)/shard_map/all_gather | solution.py:32
  16.0 0.7 convolution_bitcast_fusion.2
  16.8 19.8 %psum.21 = f32[128,80]{0,1:T(8,128)S(1)} all-reduce(f32[128,80]{0,1:T(8,128)S(1)} %convolution_bitcast_fusion.2), channel_id=1, replica_groups=mesh['lon'=8,'lat'=4] {'lat'}, use_global_device_ids=true, to_apply=%region_1.0 | all-reduce | flops 10240 | bytes 81920 | tf_op jit(solution)/shard_map/psum | solution.py:41
  36.7 0.3 convolution_add_fusion.2
  37.1 11.7 %cholesky.59 = f32[128,128]{1,0:T(8,128)S(1)} custom-call(f32[128,128]{1,0:T(8,128)S(1)} %fusion.63), custom_call_target="Cholesky" | custom-call | tf_op jit(solution)/shard_map/jit(cholesky)/cholesky | solution.py:12
  48.8 0.6 compare_reduce_fusion.2
  49.5 0.7 fusion.31
  50.1 9.8 %custom-call.16 = f32[1,128,128]{1,2,0:T(8,128)S(1)} custom-call(f32[1,128,128]{2,1,0:T(8,128)S(1)} %fusion.31), custom_call_target="InvertDiagBlocksLowerTriangular" | custom-call | tf_op jit(solution)/shard_map/jit(_cho_solve)/triangular_solve | solution.py:13
  59.9 0.3 fusion.61
  61.0 1.9 reduce_sum.54
  62.9 0.3 broadcast_subtract_fusion
  63.2 0.7 copy-done.2
  64.0 5.1 %fusion.8 = f32[128,32,256]{2,0,1:T(8,128)} fusion(f32[10,32,8,256]{3,2,1,0:T(8,128)S(1)} %bitcast.216, f32[128,256]{1,0:T(8,128)S(1)} %get-tuple-element.13, f32[128,80]{0,1:T(8,128)S(1)} %psum.21, f32[128]{0:T(128)S(1)} %get-tuple-element.18, f32[128]{0:T(128)S(1)} %broadcast_multiply_fusion.4), kind=kOutput, calls=%fused_computation.13 | convolution fusion | flops 1007712256 | bytes 6988800 | tf_op jit(solution)/shard_map/dot_general | solution.py:51
  69.1 5.6 %copy.21 = f32[128,32,256]{0,2,1:T(8,128)} copy(f32[128,32,256]{2,0,1:T(8,128)} %fusion.8) | data formatting | bytes 8388608 | tf_op jit(solution)/shard_map/mul | solution.py:52
  74.7 5.9 %fusion.34 = f32[81,8192]{1,0:T(8,128)S(1)} fusion(f32[128,8192]{0,1:T(8,128)} %bitcast.210, f32[1,128]{0,1:T(8,128)S(1)} %copy.19, f32[80,128]{0,1:T(8,128)S(1)} %fusion.15), kind=kOutput, calls=%fused_computation.62 | convolution fusion | flops 1019226240 | bytes 6889984 | tf_op jit(solution)/shard_map/dot_general | solution.py:55
  80.7 0.5 fusion.82
  81.2 1.5 copy-done
  82.6 10.1 %all-gather.1 = f32[640,256]{1,0:T(8,128)S(1)} all-gather(f32[80,256]{1,0:T(8,128)S(1)} %slice.119), channel_id=3, replica_groups=mesh['lon'=8,'lat'=4] {'lon'}, dimensions={0}, use_global_device_ids=true | all-gather | bytes 737280 | tf_op jit(solution)/shard_map/all_gather | solution.py:32
  92.8 0.7 convolution_bitcast_fusion.1
  93.6 16.3 %psum.22 = f32[128,80]{0,1:T(8,128)S(1)} all-reduce(f32[128,80]{0,1:T(8,128)S(1)} %convolution_bitcast_fusion.1), channel_id=1, replica_groups=mesh['lon'=8,'lat'=4] {'lat'}, use_global_device_ids=true, to_apply=%region_6.0 | all-reduce | flops 10240 | bytes 81920 | tf_op jit(solution)/shard_map/psum | solution.py:41
  109.9 0.3 convolution_add_fusion.1
  110.3 11.7 %cholesky.70 = f32[128,128]{1,0:T(8,128)S(1)} custom-call(f32[128,128]{1,0:T(8,128)S(1)} %fusion.57), custom_call_target="Cholesky" | custom-call | tf_op jit(solution)/shard_map/jit(cholesky)/cholesky | solution.py:12
  122.1 0.7 compare_reduce_fusion.1
  122.8 0.7 fusion.32
  123.5 9.8 %custom-call.18 = f32[1,128,128]{1,2,0:T(8,128)S(1)} custom-call(f32[1,128,128]{2,1,0:T(8,128)S(1)} %fusion.32), custom_call_target="InvertDiagBlocksLowerTriangular" | custom-call | tf_op jit(solution)/shard_map/jit(_cho_solve)/triangular_solve | solution.py:13
  133.3 0.3 fusion.55
  134.4 0.3 mul.86
  134.7 3.3 %copy.35 = f32[16,8,32,256]{3,1,2,0:T(8,128)S(1)} copy(f32[16,8,32,256]{3,2,1,0:T(8,128)S(1)} %bitcast.213) | data formatting | bytes 8388608
  138.1 4.0 %convolution_multiply_fusion.1 = f32[128,8192]{1,0:T(8,128)S(1)} fusion(f32[128,8192]{1,0:T(8,128)S(1)} %bitcast.211, f32[80,8192]{1,0:T(8,128)S(1)} %copy-done.1, f32[8192]{0:T(1024)S(1)} %broadcast_multiply_fusion.1, f32[128,80]{0,1:T(8,128)S(1)} %psum.22, f32[128]{0:T(128)S(1)} %get-tuple-element.19, f32[128]{0:T(128)S(1)} %broadcast_multiply_fusion.3), kind=kOutput, calls=%fused_computation.1 | convolution fusion | flops 1008367616 | bytes 11084800 | tf_op jit(solution)/shard_map/dot_general | solution.py:51
  142.0 3.0 %fusion.38 = f32[81,8192]{1,0:T(8,128)S(1)} fusion(f32[128,8192]{1,0:T(8,128)S(1)} %convolution_multiply_fusion.1, f32[1,128]{0,1:T(8,128)S(1)} %copy.24, f32[80,128]{0,1:T(8,128)S(1)} %fusion.14), kind=kOutput, calls=%fused_computation.66 | convolution fusion | flops 1019226240 | bytes 6889984 | tf_op jit(solution)/shard_map/dot_general | solution.py:55
  145.1 0.5 fusion.80
  145.6 9.2 %all-gather.2 = f32[640,256]{1,0:T(8,128)S(1)} all-gather(f32[80,256]{1,0:T(8,128)S(1)} %slice.122), channel_id=4, replica_groups=mesh['lon'=8,'lat'=4] {'lon'}, dimensions={0}, use_global_device_ids=true | all-gather | bytes 737280 | tf_op jit(solution)/shard_map/all_gather | solution.py:32
  154.8 0.7 convolution_bitcast_fusion
  155.6 18.1 %psum.23 = f32[128,80]{0,1:T(8,128)S(1)} all-reduce(f32[128,80]{0,1:T(8,128)S(1)} %convolution_bitcast_fusion), channel_id=1, replica_groups=mesh['lon'=8,'lat'=4] {'lat'}, use_global_device_ids=true, to_apply=%region_9.13 | all-reduce | flops 10240 | bytes 81920 | tf_op jit(solution)/shard_map/psum | solution.py:41
  173.8 0.3 convolution_add_fusion
  174.2 11.7 %cholesky.81 = f32[128,128]{1,0:T(8,128)S(1)} custom-call(f32[128,128]{1,0:T(8,128)S(1)} %fusion.51), custom_call_target="Cholesky" | custom-call | tf_op jit(solution)/shard_map/jit(cholesky)/cholesky | solution.py:12
  185.9 0.6 compare_reduce_fusion
  186.6 0.7 fusion.33
  187.2 9.8 %custom-call.20 = f32[1,128,128]{1,2,0:T(8,128)S(1)} custom-call(f32[1,128,128]{2,1,0:T(8,128)S(1)} %fusion.33), custom_call_target="InvertDiagBlocksLowerTriangular" | custom-call | tf_op jit(solution)/shard_map/jit(_cho_solve)/triangular_solve | solution.py:13
  197.1 0.3 fusion.49
  198.1 0.3 mul.93
  198.4 3.3 %copy.36 = f32[16,8,32,256]{3,1,2,0:T(8,128)S(1)} copy(f32[16,8,32,256]{3,2,1,0:T(8,128)S(1)} %bitcast.214) | data formatting | bytes 8388608
  201.7 3.8 %convolution_multiply_fusion = f32[128,8192]{1,0:T(8,128)S(1)} fusion(f32[128,8192]{1,0:T(8,128)S(1)} %bitcast.212, f32[80,8192]{1,0:T(8,128)S(1)} %get-tuple-element.8, f32[8192]{0:T(1024)S(1)} %broadcast_multiply_fusion, f32[128,80]{0,1:T(8,128)S(1)} %psum.23, f32[128]{0:T(128)S(1)} %get-tuple-element.17, f32[128]{0:T(128)S(1)} %broadcast_multiply_fusion.2), kind=kOutput, calls=%fused_computation | convolution fusion | flops 1008367616 | bytes 11084800 | tf_op jit(solution)/shard_map/dot_general | solution.py:51
  205.5 3.0 %fusion.42 = f32[81,8192]{1,0:T(8,128)S(1)} fusion(f32[128,8192]{1,0:T(8,128)S(1)} %convolution_multiply_fusion, f32[1,128]{0,1:T(8,128)S(1)} %copy.27, f32[80,128]{0,1:T(8,128)S(1)} %fusion.13), kind=kOutput, calls=%fused_computation.70 | convolution fusion | flops 1019226240 | bytes 6889984 | tf_op jit(solution)/shard_map/dot_general | solution.py:55
  208.6 0.3 fusion.3
  208.9 2.3 %copy.37 = f32[10,8,32,256]{3,2,1,0:T(8,128)} copy(f32[10,8,32,256]{3,1,2,0:T(8,128)S(1)} %bitcast.217) | data formatting | bytes 5242880
  (56 shorter events, 3.2 us)
Async XLA Ops:
  0.9 15.1 %copy-start.5 = (s32[3,128]{1,0:T(4,128)S(1)}, s32[3,128]{1,0:T(4,128)}, u32[]{:S(2)}) copy-start(s32[3,128]{1,0:T(4,128)} %param.13) | copy-start | bytes 4612
  0.9 35.8 %copy-start.3 = (f32[3,128]{1,0:T(4,128)S(1)}, f32[3,128]{1,0:T(4,128)}, u32[]{:S(2)}) copy-start(f32[3,128]{1,0:T(4,128)} %param.15) | copy-start | bytes 4612
  4.3 56.2 %copy-start.4 = (f32[3,128]{1,0:T(4,128)S(1)}, f32[3,128]{1,0:T(4,128)}, u32[]{:S(2)}) copy-start(f32[3,128]{1,0:T(4,128)} %param.14) | copy-start | bytes 4612
  62.9 1.0 copy-start.2
  81.1 1.5 copy-start
  134.7 3.4 %copy-start.1 = (f32[80,8192]{1,0:T(8,128)S(1)}, f32[80,8192]{1,0:T(8,128)}, u32[]{:S(2)}) copy-start(f32[80,8192]{1,0:T(8,128)} %copy-done) | copy-start | bytes 7864324
where the time goes:
time: 215 us; the launch traced here: 211 us
  blocking collectives  85.1 us (40%)
  other arithmetic  72.7 us (34%)
  matrix products  30.5 us (14%)
  local copies, waits for them, and re-layouts  22.4 us (10%)
    psum x3, blocking collectives, body(): obs_ens = lax.psum(row_part, 'lat')  54.3 us
    another operation x9, other arithmetic, solve_rows(): chol = jnp.linalg.cholesky(cmat)  37.2 us
    another operation x6, other arithmetic, solve_rows(): gain_rows = jax.scipy.linalg.cho_solve((chol, True), whitened)  31.4 us
    all_gather x3, blocking collectives, body(): piece = lax.all_gather(surface[None], 'lon', axis=0, tiled=True)  30.9 us
    unnamed x18, local copies, waits for them, and re-layouts  14.6 us
    dot_general x3, matrix products, body(): proj = jnp.dot(whitened, pert, precision=lax.Precision.HIGHEST)  12.9 us
    dot_general x3, matrix products, body(): incr = jnp.dot(coef, proj, precision=lax.Precision.HIGHEST)  12 us
    mul x3, local copies, waits for them, and re-layouts, body(): proj.reshape(count, levels, columns) * weights[:, None, :]  6.22 us

commit v1 on v0

--- a/solution.py
+++ b/solution.py
@@ -38,7 +38,7 @@
         row_part = jnp.zeros((count, members), jnp.float32) + jnp.einsum(
             "pkc,kmc->pm", select, piece, precision=lax.Precision.HIGHEST
         )
-        obs_ens = lax.psum(row_part, "lat")
+        obs_ens = jnp.sum(lax.all_gather(row_part, "lat"), axis=0)
         obs_mean = jnp.mean(obs_ens, axis=1)
         errors = obs_error[batch]
         whitened = (obs_ens - obs_mean[:, None]) * scale / errors[:, None]

time: 215 us -> 201 us (0.935)
  blocking collectives: 85.1 us -> 72.4 us
    psum x3 -> x0, blocking collectives: 54.3 us -> none  [body(): obs_ens = lax.psum(row_part, 'lat')]
    all_gather x0 -> x3, blocking collectives: none -> 41.5 us  [body(): obs_ens = jnp.sum(lax.all_gather(row_part, 'lat'), axis=0)]
where the time goes in v1:
time: 201 us; the launch traced here: 198 us
  other arithmetic  73.1 us (36%)
  blocking collectives  72.4 us (36%)
  matrix products  29.6 us (15%)
  local copies, waits for them, and re-layouts  22.1 us (11%)
    all_gather x3, blocking collectives, body(): obs_ens = jnp.sum(lax.all_gather(row_part, 'lat'), axis=0)  41.5 us
    another operation x9, other arithmetic, solve_rows(): chol = jnp.linalg.cholesky(cmat)  37.2 us
    another operation x6, other arithmetic, solve_rows(): gain_rows = jax.scipy.linalg.cho_solve((chol, True), whitened)  31.4 us
    all_gather x3, blocking collectives, body(): piece = lax.all_gather(surface[None], 'lon', axis=0, tiled=True)  30.8 us
    unnamed x18, local copies, waits for them, and re-layouts  14.6 us
    dot_general x3, matrix products, body(): proj = jnp.dot(whitened, pert, precision=lax.Precision.HIGHEST)  12.6 us
    dot_general x3, matrix products, body(): incr = jnp.dot(coef, proj, precision=lax.Precision.HIGHEST)  11.5 us
    mul x3, local copies, waits for them, and re-layouts, body(): proj.reshape(count, levels, columns) * weights[:, None, :]  6.24 us

profile of v1, /device:TPU:0, one launch (start us, length us, event | category | flops | bytes accessed | tf_op | source)
XLA Modules:
  0.0 198.0 jit_solution(7807502004893553199)
XLA Ops:
  0.0 0.8 slice_bitcast_fusion.2
  0.9 3.4 %copy.40 = f32[10,8,32,256]{3,1,2,0:T(8,128)S(1)} copy(f32[10,8,32,256]{3,2,1,0:T(8,128)} %bitcast.227) | data formatting | bytes 5242880
  4.3 11.6 %all-gather = f32[640,256]{1,0:T(8,128)S(1)} all-gather(f32[80,256]{1,0:T(8,128)S(1)} %slice.116), channel_id=2, replica_groups=mesh['lon'=8,'lat'=4] {'lon'}, dimensions={0}, use_global_device_ids=true | all-gather | bytes 737280 | tf_op jit(solution)/shard_map/all_gather | solution.py:32
  16.0 0.7 convolution_bitcast_fusion.2
  16.8 13.9 %all-gather.1 = f32[512,80]{0,1:T(8,128)S(1)} all-gather(f32[128,80]{0,1:T(8,128)S(1)} %convolution_bitcast_fusion.2), channel_id=3, replica_groups=mesh['lon'=8,'lat'=4] {'lat'}, dimensions={0}, use_global_device_ids=true | all-gather | bytes 204800 | tf_op jit(solution)/shard_map/all_gather | solution.py:41
  30.9 0.3 convolution_add_fusion.2
  31.3 11.7 %cholesky.59 = f32[128,128]{1,0:T(8,128)S(1)} custom-call(f32[128,128]{1,0:T(8,128)S(1)} %fusion.51), custom_call_target="Cholesky" | custom-call | tf_op jit(solution)/shard_map/jit(cholesky)/cholesky | solution.py:12
  43.1 0.6 compare_reduce_fusion.2
  43.7 0.7 fusion.31
  44.4 9.8 %custom-call.16 = f32[1,128,128]{1,2,0:T(8,128)S(1)} custom-call(f32[1,128,128]{2,1,0:T(8,128)S(1)} %fusion.31), custom_call_target="InvertDiagBlocksLowerTriangular" | custom-call | tf_op jit(solution)/shard_map/jit(_cho_solve)/triangular_solve | solution.py:13
  54.4 0.2 fusion.15
  55.0 2.0 reduce_sum.81
  57.0 0.3 broadcast_subtract_fusion
  57.3 0.7 copy-done.2
  58.0 5.1 %fusion.8 = f32[128,32,256]{2,0,1:T(8,128)} fusion(f32[10,32,8,256]{3,2,1,0:T(8,128)S(1)} %bitcast.228, f32[128,256]{1,0:T(8,128)S(1)} %get-tuple-element.13, f32[128,80]{0,1:T(8,128)S(1)} %reduce_sum.82, f32[128]{0:T(128)S(1)} %get-tuple-element.18, f32[128]{0:T(128)S(1)} %broadcast_multiply_fusion.4), kind=kOutput, calls=%fused_computation.13 | convolution fusion | flops 1007712256 | bytes 6988800 | tf_op jit(solution)/shard_map/dot_general | solution.py:51
  63.2 5.6 %copy.31 = f32[128,32,256]{0,2,1:T(8,128)} copy(f32[128,32,256]{2,0,1:T(8,128)} %fusion.8) | data formatting | bytes 8388608 | tf_op jit(solution)/shard_map/mul | solution.py:52
  68.7 6.2 %fusion.52 = f32[81,8192]{1,0:T(8,128)S(1)} fusion(f32[128,8192]{0,1:T(8,128)} %bitcast.224, f32[1,128]{1,0:T(1,128)S(1)} %fusion.21, f32[80,128]{1,0:T(8,128)S(1)} %fusion.15), kind=kOutput, calls=%fused_computation.89 | convolution fusion | flops 1019226240 | bytes 6889984 | tf_op jit(solution)/shard_map/dot_general | solution.py:55
  75.1 0.5 fusion.82
  75.5 1.5 copy-done
  77.0 10.1 %all-gather.2 = f32[640,256]{1,0:T(8,128)S(1)} all-gather(f32[80,256]{1,0:T(8,128)S(1)} %slice.119), channel_id=4, replica_groups=mesh['lon'=8,'lat'=4] {'lon'}, dimensions={0}, use_global_device_ids=true | all-gather | bytes 737280 | tf_op jit(solution)/shard_map/all_gather | solution.py:32
  87.2 0.7 convolution_bitcast_fusion.1
  88.0 13.9 %all-gather.3 = f32[512,80]{0,1:T(8,128)S(1)} all-gather(f32[128,80]{0,1:T(8,128)S(1)} %convolution_bitcast_fusion.1), channel_id=5, replica_groups=mesh['lon'=8,'lat'=4] {'lat'}, dimensions={0}, use_global_device_ids=true | all-gather | bytes 204800 | tf_op jit(solution)/shard_map/all_gather | solution.py:41
  102.0 0.3 convolution_add_fusion.1
  102.5 11.7 %cholesky.70 = f32[128,128]{1,0:T(8,128)S(1)} custom-call(f32[128,128]{1,0:T(8,128)S(1)} %fusion.45), custom_call_target="Cholesky" | custom-call | tf_op jit(solution)/shard_map/jit(cholesky)/cholesky | solution.py:12
  114.2 0.7 compare_reduce_fusion.1
  114.9 0.7 fusion.32
  115.7 9.8 %custom-call.18 = f32[1,128,128]{1,2,0:T(8,128)S(1)} custom-call(f32[1,128,128]{2,1,0:T(8,128)S(1)} %fusion.32), custom_call_target="InvertDiagBlocksLowerTriangular" | custom-call | tf_op jit(solution)/shard_map/jit(_cho_solve)/triangular_solve | solution.py:13
  125.7 0.2 fusion.14
  126.3 0.3 mul.86
  126.7 3.3 %copy.43 = f32[16,8,32,256]{3,1,2,0:T(8,128)S(1)} copy(f32[16,8,32,256]{3,2,1,0:T(8,128)S(1)} %bitcast.225) | data formatting | bytes 8388608
  130.0 3.7 %convolution_multiply_fusion.1 = f32[128,8192]{1,0:T(8,128)S(1)} fusion(f32[128,8192]{1,0:T(8,128)S(1)} %bitcast.222, f32[80,8192]{1,0:T(8,128)S(1)} %copy-done.1, f32[8192]{0:T(1024)S(1)} %broadcast_multiply_fusion.1, f32[128,80]{0,1:T(8,128)S(1)} %reduce_sum.85, f32[128]{0:T(128)S(1)} %get-tuple-element.19, f32[128]{0:T(128)S(1)} %broadcast_multiply_fusion.3), kind=kOutput, calls=%fused_computation.1 | convolution fusion | flops 1008367616 | bytes 11084800 | tf_op jit(solution)/shard_map/dot_general | solution.py:51
  133.8 2.6 %fusion.56 = f32[81,8192]{1,0:T(8,128)S(1)} fusion(f32[128,8192]{1,0:T(8,128)S(1)} %convolution_multiply_fusion.1, f32[1,128]{1,0:T(1,128)S(1)} %fusion.19, f32[80,128]{1,0:T(8,128)S(1)} %fusion.14), kind=kOutput, calls=%fused_computation.93 | convolution fusion | flops 1019226240 | bytes 6889984 | tf_op jit(solution)/shard_map/dot_general | solution.py:55
  136.4 0.5 fusion.80
  136.9 9.1 %all-gather.4 = f32[640,256]{1,0:T(8,128)S(1)} all-gather(f32[80,256]{1,0:T(8,128)S(1)} %slice.122), channel_id=6, replica_groups=mesh['lon'=8,'lat'=4] {'lon'}, dimensions={0}, use_global_device_ids=true | all-gather | bytes 737280 | tf_op jit(solution)/shard_map/all_gather | solution.py:32
  146.2 0.7 convolution_bitcast_fusion
  146.9 13.8 %all-gather.5 = f32[512,80]{0,1:T(8,128)S(1)} all-gather(f32[128,80]{0,1:T(8,128)S(1)} %convolution_bitcast_fusion), channel_id=7, replica_groups=mesh['lon'=8,'lat'=4] {'lat'}, dimensions={0}, use_global_device_ids=true | all-gather | bytes 204800 | tf_op jit(solution)/shard_map/all_gather | solution.py:41
  160.9 0.3 convolution_add_fusion
  161.3 11.7 %cholesky.81 = f32[128,128]{1,0:T(8,128)S(1)} custom-call(f32[128,128]{1,0:T(8,128)S(1)} %fusion.39), custom_call_target="Cholesky" | custom-call | tf_op jit(solution)/shard_map/jit(cholesky)/cholesky | solution.py:12
  173.0 0.6 compare_reduce_fusion
  173.7 0.7 fusion.33
  174.4 9.8 %custom-call.20 = f32[1,128,128]{1,2,0:T(8,128)S(1)} custom-call(f32[1,128,128]{2,1,0:T(8,128)S(1)} %fusion.33), custom_call_target="InvertDiagBlocksLowerTriangular" | custom-call | tf_op jit(solution)/shard_map/jit(_cho_solve)/triangular_solve | solution.py:13
  184.4 0.2 fusion.13
  185.0 0.3 mul.93
  185.4 3.3 %copy.44 = f32[16,8,32,256]{3,1,2,0:T(8,128)S(1)} copy(f32[16,8,32,256]{3,2,1,0:T(8,128)S(1)} %bitcast.226) | data formatting | bytes 8388608
  188.7 3.8 %convolution_multiply_fusion = f32[128,8192]{1,0:T(8,128)S(1)} fusion(f32[128,8192]{1,0:T(8,128)S(1)} %bitcast.223, f32[80,8192]{1,0:T(8,128)S(1)} %get-tuple-element.8, f32[8192]{0:T(1024)S(1)} %broadcast_multiply_fusion, f32[128,80]{0,1:T(8,128)S(1)} %reduce_sum.88, f32[128]{0:T(128)S(1)} %get-tuple-element.17, f32[128]{0:T(128)S(1)} %broadcast_multiply_fusion.2), kind=kOutput, calls=%fused_computation | convolution fusion | flops 1008367616 | bytes 11084800 | tf_op jit(solution)/shard_map/dot_general | solution.py:51
  192.5 2.6 %fusion.60 = f32[81,8192]{1,0:T(8,128)S(1)} fusion(f32[128,8192]{1,0:T(8,128)S(1)} %convolution_multiply_fusion, f32[1,128]{1,0:T(1,128)S(1)} %fusion.17, f32[80,128]{1,0:T(8,128)S(1)} %fusion.13), kind=kOutput, calls=%fused_computation.97 | convolution fusion | flops 1019226240 | bytes 6889984 | tf_op jit(solution)/shard_map/dot_general | solution.py:55
  195.1 0.3 fusion.3
  195.4 2.3 %copy.45 = f32[10,8,32,256]{3,2,1,0:T(8,128)} copy(f32[10,8,32,256]{3,1,2,0:T(8,128)S(1)} %bitcast.229) | data formatting | bytes 5242880
  (62 shorter events, 3.3 us)
Async XLA Ops:
  0.9 15.1 %copy-start.5 = (s32[3,128]{1,0:T(4,128)S(1)}, s32[3,128]{1,0:T(4,128)}, u32[]{:S(2)}) copy-start(s32[3,128]{1,0:T(4,128)} %param.13) | copy-start | bytes 4612
  0.9 30.0 %copy-start.3 = (f32[3,128]{1,0:T(4,128)S(1)}, f32[3,128]{1,0:T(4,128)}, u32[]{:S(2)}) copy-start(f32[3,128]{1,0:T(4,128)} %param.15) | copy-start | bytes 4612
  4.3 50.3 %copy-start.4 = (f32[3,128]{1,0:T(4,128)S(1)}, f32[3,128]{1,0:T(4,128)}, u32[]{:S(2)}) copy-start(f32[3,128]{1,0:T(4,128)} %param.14) | copy-start | bytes 4612
  57.0 1.0 copy-start.2
  75.5 1.5 copy-start
  126.7 3.4 %copy-start.1 = (f32[80,8192]{1,0:T(8,128)S(1)}, f32[80,8192]{1,0:T(8,128)}, u32[]{:S(2)}) copy-start(f32[80,8192]{1,0:T(8,128)} %copy-done) | copy-start | bytes 7864324
